TPU v7x, 256 devices: a whole 4x4x8 slice. The times are simulated.
256 devices in a mesh: section: 16 (over z, x_hi), fsdp: 16 (over x_lo, y, core).
Axes of the slice: x: 4 (x_hi: 2, x_lo: 2; x = x_hi * 2 + x_lo), y: 4, z: 8, core: 2. Of those that a mesh axis runs over, the one named last changes fastest.
Arguments:
- x_fwd: bfloat16 [16, 384, 4096], P('section', None, 'fsdp'), may hold values from -6 to 6
- x_saved: bfloat16 [16, 384, 4096], P('section', None, 'fsdp'), may hold values from -6 to 6
- cotangent: bfloat16 [16, 384, 4096], P('section', None, 'fsdp'), may hold values from -6 to 6
- qkv_weight: bfloat16 [16, 4096, 3, 4096], P('section', None, None, 'fsdp')
- gain: float32 [16, 4096], P('section', 'fsdp'), may hold values from 0.1 to 1.9
- block_lists: int32 [8, 3, 2], replicated, may hold values from 0 to 2, as said below
- plan: int32 [16, 2], P('section'), may hold values from 0 to 7
Outputs:
- y_next: bfloat16 [16, 384, 4096], P('section', None, 'fsdp')
- dx_prev: bfloat16 [16, 384, 4096], P('section', None, 'fsdp')
- w_grad: bfloat16 [16, 4096, 3, 4096], P('section', None, None, 'fsdp')
- gain_grad: float32 [16, 4096], P('section', 'fsdp')
Inputs may be any that keep to these rules, and one draw needn't show every extreme that they name: block_lists[z, b, 0] = b; the 2 entries of a row are distinct.
All inputs are finite; a program needn't handle non-finite values.
Results may differ from a plain program's by a relative error of at most 0.024.
Values may be sent and summed in bfloat16 or wider, within the bound.
No kernel may reach another device: no remote copies, remote signals or barrier semaphores. Data moves between devices by JAX's collectives and lax.ppermute only.
A program may use at most 128 MiB of HBM per device.

v0:
```python
import math
import jax
import jax.numpy as jnp
from jax import lax
from jax.sharding import PartitionSpec as P

HD = 128
BLK = 128
EPS = 1e-05


def shifted(block, axis, distance):
    devices = range(lax.axis_size(axis))
    route = [((i - distance) % len(devices), i) for i in devices]
    return lax.ppermute(block, axis, route)


def attend(query, key_in, value, block_ids):
    tokens, feat_width = query.shape
    head_count = feat_width // HD
    block_count = tokens // BLK
    band_size = block_ids.shape[1]
    q_blocks = query.reshape(block_count, BLK, head_count, HD)
    k_rows = key_in.reshape(block_count, BLK, head_count, HD)[block_ids].reshape(
        block_count, band_size * BLK, head_count, HD
    )
    v_rows = value.reshape(block_count, BLK, head_count, HD)[block_ids].reshape(
        block_count, band_size * BLK, head_count, HD
    )
    scores = jnp.einsum("qthd,qshd->qhts", q_blocks, k_rows, preferred_element_type=jnp.float32) * (
        1.0 / math.sqrt(HD)
    )
    row_max = jnp.max(scores, axis=3, keepdims=True)
    expd = jnp.exp(scores - row_max)
    probs = expd / jnp.sum(expd, axis=3, keepdims=True)
    probs_low = probs.astype(jnp.bfloat16)
    output = jnp.einsum(
        "qhts,qshd->qthd", probs_low, v_rows, preferred_element_type=jnp.float32
    ).reshape(tokens, feat_width)
    return (output, (probs, probs_low, q_blocks, k_rows, v_rows))


def attend_back(upstream, block_ids, saved):
    probs, probs_low, q_blocks, k_rows, v_rows = saved
    block_count, block_len, head_count, head_size = q_blocks.shape
    band_size = block_ids.shape[1]
    tokens = block_count * block_len
    c_blocks = upstream.reshape(block_count, block_len, head_count, head_size)
    grad_vrows = jnp.einsum(
        "qhts,qthd->qshd", probs_low, c_blocks, preferred_element_type=jnp.float32
    )
    grad_p = jnp.einsum("qthd,qshd->qhts", c_blocks, v_rows, preferred_element_type=jnp.float32)
    grad_s = (
        probs * (grad_p - jnp.sum(probs * grad_p, axis=3, keepdims=True)) * (1.0 / math.sqrt(HD))
    )
    grad_s_low = grad_s.astype(jnp.bfloat16)
    grad_q = jnp.einsum("qhts,qshd->qthd", grad_s_low, k_rows, preferred_element_type=jnp.float32)
    grad_krows = jnp.einsum(
        "qhts,qthd->qshd", grad_s_low, q_blocks, preferred_element_type=jnp.float32
    )
    onehot = (
        block_ids[:, :, None] == jnp.arange(block_count, dtype=jnp.int32)[None, None, :]
    ).astype(jnp.float32)
    band_shape = (block_count, band_size, block_len, head_count, head_size)
    grad_k = jnp.einsum("qbk,qbthd->kthd", onehot, grad_krows.reshape(band_shape))
    grad_v = jnp.einsum("qbk,qbthd->kthd", onehot, grad_vrows.reshape(band_shape))
    return (grad_q.reshape(tokens, -1), grad_k.reshape(tokens, -1), grad_v.reshape(tokens, -1))


def on_device(x_fwd, x_saved, cotangent, qkv_weight, gain, block_lists, plan):
    forward_in = x_fwd[0]
    saved_in = x_saved[0]
    upstream = cotangent[0]
    weight = qkv_weight[0]
    gain_row = gain[0]
    full_width = weight.shape[0]
    local = weight.shape[2]
    tokens = forward_in.shape[0]
    w_flat = weight.reshape(full_width, 3 * local)
    lists_fwd = block_lists[plan[0, 0]]
    lists_bwd = block_lists[plan[0, 1]]
    wide_fwd = forward_in.astype(jnp.float32)
    wide_bwd = saved_in.astype(jnp.float32)
    scaled_fwd = (wide_fwd * gain_row[None, :]).astype(jnp.bfloat16)
    scaled_bwd = (wide_bwd * gain_row[None, :]).astype(jnp.bfloat16)
    sq_fwd, sq_bwd = lax.psum(
        (jnp.sum(wide_fwd * wide_fwd, axis=1), jnp.sum(wide_bwd * wide_bwd, axis=1)), "fsdp"
    )
    scale_fwd = lax.rsqrt(sq_fwd / full_width + EPS)
    scale_bwd = lax.rsqrt(sq_bwd / full_width + EPS)
    product_fwd = jnp.dot(
        lax.all_gather(scaled_fwd, "fsdp", axis=1, tiled=True),
        w_flat,
        preferred_element_type=jnp.float32,
    )
    whole_bwd = lax.all_gather(scaled_bwd, "fsdp", axis=1, tiled=True)
    product_bwd = jnp.dot(whole_bwd, w_flat, preferred_element_type=jnp.float32)
    proj_fwd = (scale_fwd[:, None] * product_fwd).astype(jnp.bfloat16)
    attn_fwd = attend(
        proj_fwd[:, :local], proj_fwd[:, local : 2 * local], proj_fwd[:, 2 * local :], lists_fwd
    )[0]
    result = (wide_fwd + attn_fwd).astype(jnp.bfloat16)
    sent_on = shifted(result[None], "section", 1)
    proj_bwd = (scale_bwd[:, None] * product_bwd).astype(jnp.bfloat16)
    saved = attend(
        proj_bwd[:, :local], proj_bwd[:, local : 2 * local], proj_bwd[:, 2 * local :], lists_bwd
    )[1]
    grad_q, grad_k, grad_v = attend_back(upstream, lists_bwd, saved)
    stacked = jnp.stack([grad_q, grad_k, grad_v], axis=1).reshape(tokens, 3 * local)
    grads = (scale_bwd[:, None] * stacked).astype(jnp.bfloat16)
    grad_w = lax.dot_general(
        whole_bwd, grads, (((0,), (0,)), ((), ())), preferred_element_type=jnp.float32
    )
    grad_w = grad_w.astype(jnp.bfloat16).reshape(1, full_width, 3, local)
    partial_in = lax.dot_general(
        grads, w_flat, (((1,), (1,)), ((), ())), preferred_element_type=jnp.float32
    )
    summed_in = lax.psum(partial_in.astype(jnp.bfloat16), "fsdp").astype(jnp.float32)
    own_in = lax.dynamic_slice_in_dim(summed_in, lax.axis_index("fsdp") * local, local, 1)
    row_total = jnp.sum(whole_bwd.astype(jnp.float32) * summed_in, axis=1)
    grad_x = upstream.astype(jnp.float32) + gain_row[None, :] * own_in
    grad_x = grad_x - (scale_bwd * scale_bwd * row_total / full_width)[:, None] * wide_bwd
    sent_back = shifted(grad_x.astype(jnp.bfloat16)[None], "section", -1)
    grad_gain = jnp.sum(wide_bwd * own_in, axis=0)[None]
    return (sent_on, sent_back, grad_w, grad_gain)


def solution(mesh):
    in_specs = (
        P("section", None, "fsdp"),
        P("section", None, "fsdp"),
        P("section", None, "fsdp"),
        P("section", None, None, "fsdp"),
        P("section", "fsdp"),
        P(),
        P("section", None),
    )
    out_specs = (
        P("section", None, "fsdp"),
        P("section", None, "fsdp"),
        P("section", None, None, "fsdp"),
        P("section", "fsdp"),
    )
    return jax.shard_map(
        on_device, mesh=mesh, in_specs=in_specs, out_specs=out_specs, check_vma=False
    )
```

profile of v0, /device:TPU:25, one launch (start us, length us, event | category | flops | bytes accessed | tf_op | source)
XLA Modules:
  0.0 275.0 jit_solution(14417627607529717031)
XLA Ops:
  7.2 1.9 fusion.21
  9.1 0.7 all-gather.3.cloned.1.call-update
  9.9 1.3 fusion.70
  13.7 8.7 %copy.55 = bf16[1,4096,3,256]{1,3,2,0:T(8,128)(2,1)} copy(bf16[1,4096,3,256]{3,1,2,0:T(8,128)(2,1)} %param.10) | data formatting | bytes 12582912 | tf_op args[3]
  24.1 26.6 %all-reduce = (f32[384]{0:T(512)S(1)}, f32[384]{0:T(512)S(1)}) all-reduce(f32[384]{0:T(512)S(1)} %get-tuple-element.28, f32[384]{0:T(512)S(1)} %get-tuple-element.32), channel_id=1, replica_groups=mesh['section'=16,'fsdp'=16] {'fsdp'}, use_global_device_ids=true, to_apply=%region_1.0 | all-reduce | flops 768 | bytes 6144 | tf_op jit(solution)/shard_map/psum | solution.py:86
  50.7 5.6 %all-gather.5.cloned.1.call-done = bf16[384,4096]{1,0:T(8,128)(2,1)} async-done(((bf16[384,256]{1,0:T(8,128)(2,1)}), bf16[384,4096]{1,0:T(8,128)(2,1)}) %all-gather.5.cloned.1.call-update) | async-done | bytes 3145744 | tf_op jit(solution)/shard_map/all_gather | solution.py:96
  56.3 6.4 %fusion.6 = bf16[384,768]{1,0:T(8,128)(2,1)S(1)} fusion(bf16[384,4096]{1,0:T(8,128)(2,1)} %all-gather.5.cloned.1.call-done, bf16[4096,768]{0,1:T(8,128)(2,1)} %bitcast.81, f32[384]{0:T(512)S(1)} %add_rsqrt_fusion), kind=kOutput, calls=%fused_computation.15 | convolution fusion | flops 2416508928 | bytes 10028544 | tf_op jit(solution)/shard_map/dot_general | solution.py:97
  62.8 0.6 gather_fusion.3
  63.6 0.6 gather_fusion.2
  64.3 0.2 copy.80
  64.5 0.3 convolution_bitcast_fusion.1
  64.8 1.3 fusion.76
  66.1 5.9 %convolution_bitcast_fusion.4 = f32[3,128,2,128]{1,3,2,0:T(8,128)S(1)} fusion(f32[3,2,128,256]{3,2,1,0:T(8,128)S(1)} %convolution_bitcast_fusion.1, bf16[3,256,2,128]{3,1,0,2:T(8,128)(2,1)S(1)} %bitcast.91, f32[3,2,128,256]{3,2,1,0:T(8,128)} %get-tuple-element.37, f32[3,2,128]{2,1,0:T(2,128)S(1)} %get-tuple-element.36), kind=kOutput, calls=%fused_computation.28 | convolution fusion | flops 51708928 | bytes 2362368 | tf_op jit(solution)/shard_map/qhts,qshd->qthd/dot_general | solution.py:57
  72.0 0.2 copy.78
  72.2 0.3 stack_reshape.9
  72.5 5.4 %convolution_bitcast_fusion = bf16[3,256,2,128]{1,3,2,0:T(8,128)(2,1)S(1)} fusion(bf16[3,128,2,128]{1,3,2,0:T(8,128)(2,1)S(1)} %copy.80, f32[3,2,128,256]{3,2,1,0:T(8,128)S(1)} %convolution_bitcast_fusion.1, f32[3,2,128,256]{3,2,1,0:T(8,128)} %get-tuple-element.37, f32[3,2,128]{2,1,0:T(2,128)S(1)} %get-tuple-element.36), kind=kOutput, calls=%fused_computation.21 | convolution fusion | flops 51708928 | bytes 2165760 | tf_op jit(solution)/shard_map/qhts,qthd->qshd/dot_general | solution.py:58
  78.0 0.7 copy.81
  78.7 0.5 convolution_bitcast_fusion.3
  79.2 0.2 copy.82
  79.4 0.3 stack_reshape.10
  79.8 1.7 fusion.32
  81.5 0.6 convolution_bitcast_fusion.2
  82.1 0.2 copy.86
  82.3 0.3 stack_reshape.11
  82.9 0.3 copy.87
  83.2 7.1 %convolution_convert_fusion.1 = bf16[384,4096]{1,0:T(8,128)(2,1)} fusion(bf16[384,768]{0,1:T(8,128)(2,1)S(1)} %bitcast.86, bf16[4096,768]{0,1:T(8,128)(2,1)} %bitcast.82), kind=kOutput, calls=%fused_computation.9 | convolution fusion | flops 2417491968 | bytes 10027008 | tf_op jit(solution)/shard_map/dot_general | solution.py:115
  90.6 0.4 copy.88
  90.9 11.8 %all-gather.3.cloned.1.call-done = bf16[384,4096]{1,0:T(8,128)(2,1)} async-done(((bf16[384,256]{1,0:T(8,128)(2,1)}), bf16[384,4096]{1,0:T(8,128)(2,1)}) %all-gather.3.cloned.1.call-update) | async-done | bytes 3145744 | tf_op jit(solution)/shard_map/all_gather | solution.py:92
  102.7 6.4 %fusion.5 = bf16[384,768]{1,0:T(8,128)(2,1)S(1)} fusion(bf16[384,4096]{1,0:T(8,128)(2,1)} %all-gather.3.cloned.1.call-done, bf16[4096,768]{0,1:T(8,128)(2,1)} %bitcast.83, f32[384]{0:T(512)S(1)} %add_rsqrt_fusion.1), kind=kOutput, calls=%fused_computation.14 | convolution fusion | flops 2416508928 | bytes 10028544 | tf_op jit(solution)/shard_map/dot_general | solution.py:91
  109.2 0.6 gather_fusion
  109.9 0.8 copy.59
  110.7 0.6 gather_fusion.1
  111.5 0.5 fusion.71
  112.0 0.3 convolution_multiply_fusion.3
  112.4 1.6 convolution_bitcast_fusion.5
  114.0 0.2 copy.65
  114.2 0.3 reshape.154
  114.6 3.2 %collective-permute-start = (bf16[1,384,256]{2,1,0:T(8,128)(2,1)S(1)}, bf16[1,384,256]{2,1,0:T(8,128)(2,1)S(1)}, u32[]{:S(2)}, u32[]{:S(2)}) collective-permute-start(bf16[1,384,256]{2,1,0:T(8,128)(2,1)S(1)} %fusion.23), channel_id=1, source_target_pairs={{240,0},{0,16},{16,32},{32,48},{48,64},{64,80},{80,96},{96,112},{1... | collective-permute-start | bytes 589832 | tf_op jit(solution)/shard_map/ppermute | solution.py:15
  117.8 0.4 copy.89
  118.2 123.7 %all-reduce.3.cloned.1.call-done = bf16[384,4096]{1,0:T(8,128)(2,1)} async-done(((bf16[384,4096]{1,0:T(8,128)(2,1)}), bf16[384,4096]{1,0:T(8,128)(2,1)}) %all-reduce.3.cloned.1.call-update) | async-done | bytes 3145744 | tf_op jit(solution)/shard_map/psum | solution.py:118
  241.9 3.9 %multiply_reduce_fusion = f32[384]{0:T(512)S(1)} fusion(bf16[384,4096]{1,0:T(8,128)(2,1)} %all-gather.5.cloned.1.call-done, bf16[384,4096]{1,0:T(8,128)(2,1)} %all-reduce.3.cloned.1.call-done), kind=kLoop, calls=%fused_computation.8 | loop fusion | flops 6291072 | bytes 6292992 | tf_op jit(solution)/shard_map/reduce_sum | solution.py:120
  245.8 0.8 convert_element_type.94
  246.7 0.7 fusion.28
  247.4 5.4 %collective-permute-start.1 = (bf16[1,384,256]{2,1,0:T(8,128)(2,1)S(1)}, bf16[1,384,256]{2,1,0:T(8,128)(2,1)S(1)}, u32[]{:S(2)}, u32[]{:S(2)}) collective-permute-start(bf16[1,384,256]{2,1,0:T(8,128)(2,1)S(1)} %get-tuple-element.19), channel_id=1, source_target_pairs={{16,0},{32,16},{48,32},{64,48},{80,64},{96,80},{112,96},{128,112},... | collective-permute-start | bytes 589832 | tf_op jit(solution)/shard_map/ppermute | solution.py:15
  252.9 5.6 %convolution_convert_fusion = bf16[4096,768]{0,1:T(8,128)(2,1)} fusion(bf16[384,4096]{1,0:T(8,128)(2,1)S(1)} %copy-done.1, f32[384,768]{1,0:T(8,128)S(1)} %copy.89, f32[384]{0:T(512)S(1)} %add_rsqrt_fusion), kind=kOutput, calls=%fused_computation.7 | convolution fusion | flops 2419654656 | bytes 10618368 | tf_op jit(solution)/shard_map/dot_general | solution.py:111
  258.5 8.6 %copy.90 = bf16[1,4096,3,256]{3,1,2,0:T(8,128)(2,1)} copy(bf16[1,4096,3,256]{1,3,2,0:T(8,128)(2,1)} %bitcast.84) | data formatting | bytes 12582912
  267.1 0.7 copy.141
  267.8 0.7 copy.142
  (58 shorter events, 2.1 us)
Async XLA Ops:
  7.2 49.1 %all-gather.5.cloned.1.call-start = ((), (), s32[]{:S(2)}) async-start(), calls=%async_computation.1 | async-start | bytes 3342336 | tf_op jit(solution)/shard_map/all_gather | solution.py:96
  9.1 93.6 %all-gather.3.cloned.1.call-start = ((), (), s32[]{:S(2)}) async-start(), calls=%async_computation | async-start | bytes 3342336 | tf_op jit(solution)/shard_map/all_gather | solution.py:92
  9.8 232.1 %all-reduce.3.cloned.1.call-start = ((), (), s32[]{:S(2)}) async-start(), calls=%async_computation.2 | async-start | bytes 6291456 | tf_op jit(solution)/shard_map/psum | solution.py:118
  13.6 9.9 %copy-start.6 = (s32[8,3,2]{0,2,1:T(2,128)S(1)}, s32[8,3,2]{0,2,1:T(2,128)}, u32[]{:S(2)}) copy-start(s32[8,3,2]{0,2,1:T(2,128)} %param.12) | copy-start | bytes 580
  13.7 10.4 %copy-start.2 = (bf16[1,384,256]{2,1,0:T(8,128)(2,1)S(1)}, bf16[1,384,256]{2,1,0:T(8,128)(2,1)}, u32[]{:S(2)}) copy-start(bf16[1,384,256]{2,1,0:T(8,128)(2,1)} %param.9) | copy-start | bytes 589828
  111.4 1.0 copy-start.5
  111.9 2.6 copy-start.4
  114.6 152.4 %collective-permute-start = (bf16[1,384,256]{2,1,0:T(8,128)(2,1)S(1)}, bf16[1,384,256]{2,1,0:T(8,128)(2,1)S(1)}, u32[]{:S(2)}, u32[]{:S(2)}) collective-permute-start(bf16[1,384,256]{2,1,0:T(8,128)(2,1)S(1)} %fusion.23), channel_id=1, source_target_pairs={{240,0},{0,16},{16,32},{32,48},{48,64},{64,80},{80,96},{96,112},{1... | collective-permute-start | bytes 589832 | tf_op jit(solution)/shard_map/ppermute | solution.py:15
  241.9 3.9 %copy-start = (bf16[384,4096]{1,0:T(8,128)(2,1)S(1)}, bf16[384,4096]{1,0:T(8,128)(2,1)}, u32[]{:S(2)}) copy-start(bf16[384,4096]{1,0:T(8,128)(2,1)} %all-reduce.3.cloned.1.call-done) | copy-start | bytes 9437188
  245.8 0.9 copy-start.3
  245.8 0.9 copy-start.7
  245.8 7.1 %copy-start.1 = (bf16[384,4096]{1,0:T(8,128)(2,1)S(1)}, bf16[384,4096]{1,0:T(8,128)(2,1)}, u32[]{:S(2)}) copy-start(bf16[384,4096]{1,0:T(8,128)(2,1)} %all-gather.5.cloned.1.call-done) | copy-start | bytes 9437188
  247.4 19.6 %collective-permute-start.1 = (bf16[1,384,256]{2,1,0:T(8,128)(2,1)S(1)}, bf16[1,384,256]{2,1,0:T(8,128)(2,1)S(1)}, u32[]{:S(2)}, u32[]{:S(2)}) collective-permute-start(bf16[1,384,256]{2,1,0:T(8,128)(2,1)S(1)} %get-tuple-element.19), channel_id=1, source_target_pairs={{16,0},{32,16},{48,32},{64,48},{80,64},{96,80},{112,96},{128,112},... | collective-permute-start | bytes 589832 | tf_op jit(solution)/shard_map/ppermute | solution.py:15
Sparse Core Ops, SparseCore 0:
  10.3 45.9 all-gather.4
  58.7 44.0 all-gather.2
  105.4 136.4 all-reduce.2
where the time goes:
time: 276 us; the launch traced here: 275 us
  waiting for transfers between devices  142 us (51%)
  matrix products  43.6 us (16%)
  local copies, waits for them, and re-layouts  29 us (11%)
  blocking collectives  26.6 us (10%)
  between operations  17.8 us (6%)
  starting transfers between devices  8.75 us (3%)
  other arithmetic  7.41 us (3%)
    psum x1, waiting for transfers between devices, on_device(): lax.psum(partial_in.astype(jnp.bfloat16), 'fsdp').astype(jnp.float32)  124 us
    psum x1, blocking collectives, on_device(): lax.psum((jnp.sum(wide_fwd * wide_fwd, axis=1), jnp.sum(wide_bwd * wide_b...  26.6 us
    unnamed x22, local copies, waits for them, and re-layouts  19 us
    all_gather x1, waiting for transfers between devices, on_device(): lax.all_gather(scaled_fwd, 'fsdp', axis=1, tiled=True)  11.8 us
    ppermute x2, starting transfers between devices, shifted(): return lax.ppermute(block, axis, route)  8.63 us
    dot_general x1, matrix products, on_device(): lax.dot_general(grads, w_flat, (((1,), (1,)), ((), ())), preferred_elemen...  7.14 us
    dot_general x1, matrix products, on_device(): jnp.dot(lax.all_gather(scaled_fwd, 'fsdp', axis=1, tiled=True), w_flat, p...  6.37 us
    dot_general x1, matrix products, on_device(): product_bwd = jnp.dot(whole_bwd, w_flat, preferred_element_type=jnp.float32)  6.37 us
  transfers between devices with their start and end apart: 5, of which 3 were waited for; matrix products, arithmetic and copies ran while one was open for 28% of the time, Pallas kernels for 0%

commit v1 on v0

--- a/solution.py
+++ b/solution.py
@@ -115,7 +115,9 @@
     partial_in = lax.dot_general(
         grads, w_flat, (((1,), (1,)), ((), ())), preferred_element_type=jnp.float32
     )
-    summed_in = lax.psum(partial_in.astype(jnp.bfloat16), "fsdp").astype(jnp.float32)
+    summed_in = jnp.sum(lax.all_gather(partial_in.astype(jnp.bfloat16), "fsdp"), axis=0).astype(
+        jnp.float32
+    )
     own_in = lax.dynamic_slice_in_dim(summed_in, lax.axis_index("fsdp") * local, local, 1)
     row_total = jnp.sum(whole_bwd.astype(jnp.float32) * summed_in, axis=1)
     grad_x = upstream.astype(jnp.float32) + gain_row[None, :] * own_in

time: 276 us -> 411 us (1.49)
  waiting for transfers between devices: 142 us -> 260 us
  other arithmetic: 7.41 us -> 21.9 us
    all_gather x0 -> x1, waiting for transfers between devices: none -> 243 us  [on_device(): lax.all_gather(partial_in.astype(jnp.bfloat16), 'fsdp')]
    psum x1 -> x0, waiting for transfers between devices: 124 us -> none  [on_device(): lax.psum(partial_in.astype(jnp.bfloat16), 'fsdp').astype(jnp.float32)]
    reduce_sum x0 -> x1, other arithmetic: none -> 16.7 us  [on_device(): jnp.sum(lax.all_gather(partial_in.astype(jnp.bfloat16), 'fsdp'), axis=0)]
  transfers between devices with their start and end apart: 5 -> 5, of which waited for: 3 -> 3; matrix products, arithmetic and copies ran while one was open for 28% -> 22% of each run, Pallas kernels for 0% -> 0%
where the time goes in v1:
time: 411 us; the launch traced here: 410 us
  waiting for transfers between devices  260 us (63%)
  matrix products  43.6 us (11%)
  local copies, waits for them, and re-layouts  31 us (8%)
  blocking collectives  26.6 us (6%)
  other arithmetic  21.9 us (5%)
  between operations  18.2 us (4%)
  starting transfers between devices  8.12 us (2%)
    all_gather x1, waiting for transfers between devices, on_device(): lax.all_gather(partial_in.astype(jnp.bfloat16), 'fsdp')  243 us
    psum x1, blocking collectives, on_device(): lax.psum((jnp.sum(wide_fwd * wide_fwd, axis=1), jnp.sum(wide_bwd * wide_b...  26.6 us
    unnamed x22, local copies, waits for them, and re-layouts  20 us
    reduce_sum x1, other arithmetic, on_device(): jnp.sum(lax.all_gather(partial_in.astype(jnp.bfloat16), 'fsdp'), axis=0)  16.7 us
    all_gather x1, waiting for transfers between devices, on_device(): lax.all_gather(scaled_fwd, 'fsdp', axis=1, tiled=True)  11.9 us
  transfers between devices with their start and end apart: 5, of which 3 were waited for; matrix products, arithmetic and copies ran while one was open for 22% of the time, Pallas kernels for 0%

profile of v1, /device:TPU:25, one launch (start us, length us, event | category | flops | bytes accessed | tf_op | source)
XLA Modules:
  0.0 409.8 jit_solution(213890932307727277)
XLA Ops:
  7.2 1.9 fusion.21
  9.1 0.7 all-gather.5.cloned.1.call-update
  9.9 1.3 fusion.70
  13.9 8.7 %copy.55 = bf16[1,4096,3,256]{1,3,2,0:T(8,128)(2,1)} copy(bf16[1,4096,3,256]{3,1,2,0:T(8,128)(2,1)} %param.10) | data formatting | bytes 12582912 | tf_op args[3]
  24.5 26.6 %all-reduce = (f32[384]{0:T(512)S(1)}, f32[384]{0:T(512)S(1)}) all-reduce(f32[384]{0:T(512)S(1)} %get-tuple-element.28, f32[384]{0:T(512)S(1)} %get-tuple-element.32), channel_id=1, replica_groups=mesh['section'=16,'fsdp'=16] {'fsdp'}, use_global_device_ids=true, to_apply=%region_1.0 | all-reduce | flops 768 | bytes 6144 | tf_op jit(solution)/shard_map/psum | solution.py:86
  51.1 5.1 %all-gather.7.cloned.1.call-done = bf16[384,4096]{1,0:T(8,128)(2,1)} async-done(((bf16[384,256]{1,0:T(8,128)(2,1)}), bf16[384,4096]{1,0:T(8,128)(2,1)}) %all-gather.7.cloned.1.call-update) | async-done | bytes 3145744 | tf_op jit(solution)/shard_map/all_gather | solution.py:96
  56.2 6.4 %fusion.6 = bf16[384,768]{1,0:T(8,128)(2,1)S(1)} fusion(bf16[384,4096]{1,0:T(8,128)(2,1)} %all-gather.7.cloned.1.call-done, bf16[4096,768]{0,1:T(8,128)(2,1)} %bitcast.83, f32[384]{0:T(512)S(1)} %add_rsqrt_fusion), kind=kOutput, calls=%fused_computation.15 | convolution fusion | flops 2416508928 | bytes 10028544 | tf_op jit(solution)/shard_map/dot_general | solution.py:97
  62.7 0.6 gather_fusion.3
  63.4 0.6 gather_fusion.2
  64.3 0.3 convolution_bitcast_fusion.1
  64.6 1.3 fusion.76
  65.9 5.9 %convolution_bitcast_fusion.4 = f32[3,128,2,128]{1,3,2,0:T(8,128)S(1)} fusion(f32[3,2,128,256]{3,2,1,0:T(8,128)S(1)} %convolution_bitcast_fusion.1, bf16[3,256,2,128]{3,1,0,2:T(8,128)(2,1)S(1)} %bitcast.93, f32[3,2,128,256]{3,2,1,0:T(8,128)} %get-tuple-element.37, f32[3,2,128]{2,1,0:T(2,128)S(1)} %get-tuple-element.36), kind=kOutput, calls=%fused_computation.28 | convolution fusion | flops 51708928 | bytes 2362368 | tf_op jit(solution)/shard_map/qhts,qshd->qthd/dot_general | solution.py:57
  71.8 0.2 copy.78
  72.1 0.3 stack_reshape.9
  72.4 5.4 %convolution_bitcast_fusion = bf16[3,256,2,128]{1,3,2,0:T(8,128)(2,1)S(1)} fusion(bf16[3,128,2,128]{1,3,2,0:T(8,128)(2,1)S(1)} %copy.80, f32[3,2,128,256]{3,2,1,0:T(8,128)S(1)} %convolution_bitcast_fusion.1, f32[3,2,128,256]{3,2,1,0:T(8,128)} %get-tuple-element.37, f32[3,2,128]{2,1,0:T(2,128)S(1)} %get-tuple-element.36), kind=kOutput, calls=%fused_computation.21 | convolution fusion | flops 51708928 | bytes 2165760 | tf_op jit(solution)/shard_map/qhts,qthd->qshd/dot_general | solution.py:58
  77.8 0.7 copy.81
  78.6 0.5 convolution_bitcast_fusion.3
  79.3 0.3 stack_reshape.10
  79.6 1.7 fusion.32
  81.3 0.6 convolution_bitcast_fusion.2
  82.2 0.3 stack_reshape.11
  82.7 0.3 copy.87
  83.0 7.2 %convolution_convert_fusion.1 = bf16[384,4096]{1,0:T(8,128)(2,1)} fusion(bf16[384,768]{0,1:T(8,128)(2,1)S(1)} %bitcast.88, bf16[4096,768]{0,1:T(8,128)(2,1)} %bitcast.84), kind=kOutput, calls=%fused_computation.9 | convolution fusion | flops 2417491968 | bytes 10027008 | tf_op jit(solution)/shard_map/dot_general | solution.py:115
  90.5 0.4 copy.88
  90.9 11.9 %all-gather.5.cloned.1.call-done = bf16[384,4096]{1,0:T(8,128)(2,1)} async-done(((bf16[384,256]{1,0:T(8,128)(2,1)}), bf16[384,4096]{1,0:T(8,128)(2,1)}) %all-gather.5.cloned.1.call-update) | async-done | bytes 3145744 | tf_op jit(solution)/shard_map/all_gather | solution.py:92
  102.8 6.4 %fusion.5 = bf16[384,768]{1,0:T(8,128)(2,1)S(1)} fusion(bf16[384,4096]{1,0:T(8,128)(2,1)} %all-gather.5.cloned.1.call-done, bf16[4096,768]{0,1:T(8,128)(2,1)} %bitcast.85, f32[384]{0:T(512)S(1)} %add_rsqrt_fusion.1), kind=kOutput, calls=%fused_computation.14 | convolution fusion | flops 2416508928 | bytes 10028544 | tf_op jit(solution)/shard_map/dot_general | solution.py:91
  109.3 0.6 gather_fusion
  109.9 0.8 copy.59
  110.8 0.6 gather_fusion.1
  111.5 0.5 fusion.71
  112.0 0.3 convolution_multiply_fusion.3
  112.4 1.6 convolution_bitcast_fusion.5
  114.1 0.2 copy.65
  114.3 0.3 reshape.154
  114.6 0.7 fusion.23
  115.4 2.7 collective-permute-start
  118.1 1.4 copy.89
  119.5 242.6 %all-gather.9.cloned.1.call-done = bf16[6144,4096]{1,0:T(8,128)(2,1)} async-done(((bf16[384,4096]{1,0:T(8,128)(2,1)}), bf16[6144,4096]{1,0:T(8,128)(2,1)}) %all-gather.9.cloned.1.call-update) | async-done | bytes 50331664 | tf_op jit(solution)/shard_map/all_gather | solution.py:118
  362.1 16.7 %reduce_sum.80 = bf16[384,4096]{1,0:T(8,128)(2,1)S(1)} reduce(bf16[16,384,4096]{2,1,0:T(8,128)(2,1)} %bitcast.82, bf16[]{:T(256)} %constant.26.clone.1), dimensions={0}, to_apply=%region_9.0 | reduce | flops 23592960 | bytes 53477376 | tf_op jit(solution)/shard_map/reduce_sum | solution.py:118
  378.8 0.8 convert_element_type.96
  379.6 1.1 copy-done
  380.7 1.0 multiply_reduce_fusion
  381.8 0.7 fusion.28
  382.5 5.3 %collective-permute-start.1 = (bf16[1,384,256]{2,1,0:T(8,128)(2,1)S(1)}, bf16[1,384,256]{2,1,0:T(8,128)(2,1)S(1)}, u32[]{:S(2)}, u32[]{:S(2)}) collective-permute-start(bf16[1,384,256]{2,1,0:T(8,128)(2,1)S(1)} %get-tuple-element.19), channel_id=1, source_target_pairs={{16,0},{32,16},{48,32},{64,48},{80,64},{96,80},{112,96},{128,112},... | collective-permute-start | bytes 589832 | tf_op jit(solution)/shard_map/ppermute | solution.py:15
  387.7 5.6 %convolution_convert_fusion = bf16[4096,768]{0,1:T(8,128)(2,1)} fusion(bf16[384,4096]{1,0:T(8,128)(2,1)S(1)} %copy-done, f32[384,768]{1,0:T(8,128)S(1)} %copy-done.1, f32[384]{0:T(512)S(1)} %add_rsqrt_fusion), kind=kOutput, calls=%fused_computation.7 | convolution fusion | flops 2419654656 | bytes 10618368 | tf_op jit(solution)/shard_map/dot_general | solution.py:111
  393.3 8.6 %copy.90 = bf16[1,4096,3,256]{3,1,2,0:T(8,128)(2,1)} copy(bf16[1,4096,3,256]{1,3,2,0:T(8,128)(2,1)} %bitcast.86) | data formatting | bytes 12582912
  401.9 0.7 copy.140
  402.6 0.7 copy.141
  (59 shorter events, 2.5 us)
Async XLA Ops:
  7.2 49.0 %all-gather.7.cloned.1.call-start = ((), (), s32[]{:S(2)}) async-start(), calls=%async_computation.1 | async-start | bytes 3342336 | tf_op jit(solution)/shard_map/all_gather | solution.py:96
  9.1 93.7 %all-gather.5.cloned.1.call-start = ((), (), s32[]{:S(2)}) async-start(), calls=%async_computation | async-start | bytes 3342336 | tf_op jit(solution)/shard_map/all_gather | solution.py:92
  9.8 352.3 %all-gather.9.cloned.1.call-start = ((), (), s32[]{:S(2)}) async-start(), calls=%async_computation.2 | async-start | bytes 53477376 | tf_op jit(solution)/shard_map/all_gather | solution.py:118
  13.9 10.0 %copy-start.6 = (s32[8,3,2]{0,2,1:T(2,128)S(1)}, s32[8,3,2]{0,2,1:T(2,128)}, u32[]{:S(2)}) copy-start(s32[8,3,2]{0,2,1:T(2,128)} %param.12) | copy-start | bytes 580
  13.9 10.5 %copy-start.2 = (bf16[1,384,256]{2,1,0:T(8,128)(2,1)S(1)}, bf16[1,384,256]{2,1,0:T(8,128)(2,1)}, u32[]{:S(2)}) copy-start(bf16[1,384,256]{2,1,0:T(8,128)(2,1)} %param.9) | copy-start | bytes 589828
  111.4 1.0 copy-start.5
  112.0 2.6 copy-start.4
  115.4 286.5 %collective-permute-start = (bf16[1,384,256]{2,1,0:T(8,128)(2,1)}, bf16[1,384,256]{2,1,0:T(8,128)(2,1)S(1)}, u32[]{:S(2)}, u32[]{:S(2)}) collective-permute-start(bf16[1,384,256]{2,1,0:T(8,128)(2,1)} %fusion.23), channel_id=1, source_target_pairs={{240,0},{0,16},{16,32},{32,48},{48,64},{64,80},{80,96},{96,112},{1... | collective-permute-start | bytes 589832 | tf_op jit(solution)/shard_map/ppermute | solution.py:15
  378.8 1.9 copy-start
  380.7 1.0 copy-start.3
  380.7 1.0 copy-start.7
  380.7 7.0 %copy-start.1 = (f32[384,768]{1,0:T(8,128)S(1)}, f32[384,768]{1,0:T(8,128)}, u32[]{:S(2)}) copy-start(f32[384,768]{1,0:T(8,128)} %copy.89) | copy-start | bytes 3538948
  382.5 19.4 %collective-permute-start.1 = (bf16[1,384,256]{2,1,0:T(8,128)(2,1)S(1)}, bf16[1,384,256]{2,1,0:T(8,128)(2,1)S(1)}, u32[]{:S(2)}, u32[]{:S(2)}) collective-permute-start(bf16[1,384,256]{2,1,0:T(8,128)(2,1)S(1)} %get-tuple-element.19), channel_id=1, source_target_pairs={{16,0},{32,16},{48,32},{64,48},{80,64},{96,80},{112,96},{128,112},... | collective-permute-start | bytes 589832 | tf_op jit(solution)/shard_map/ppermute | solution.py:15
Sparse Core Ops, SparseCore 0:
  10.3 45.7 all-gather.6
  58.5 44.2 all-gather.4
  104.6 257.4 all-gather.8
